TPU v7x, 512 devices: a whole 4x4x16 slice. The times are simulated.
512 devices in a mesh: stn: 64 (over x, y, z_hi, core), chan: 8 (over z_lo).
Axes of the slice: x: 4, y: 4, z: 16 (z_hi: 2, z_lo: 8; z = z_hi * 8 + z_lo), core: 2. Of those that a mesh axis runs over, the one named last changes fastest.
Arguments:
- voltages: bfloat16 [512, 2, 2, 8, 4864], P('stn', None, None, 'chan'), may hold values from -6 to 6
- prototype: float32 [16, 256], replicated, may hold values from -1.5 to 1.5
- kernel_table: float32 [8, 7], replicated, may hold values from 0.05 to 1
- tile_subgrid: int32 [8, 512, 4, 512, 1], P('chan', 'stn'), may hold values from 0 to 31; in each aligned block of 16384 rows (0 to 16383, 16384 to 32767, ..., all dimensions but the last counted through in order) at most 1024 rows name the same one
- tile_cells: int32 [8, 512, 4, 512, 2], P('chan', 'stn'), may hold values from 3 to 44
- tile_offsets: int32 [8, 512, 4, 512, 2], P('chan', 'stn'), may hold values from 0 to 7
- subgrid_slot: int32 [32], replicated, may hold values from 0 to 31, each once
Outputs:
- uv_grid: float32 [32, 48, 384], P('chan', None, 'stn')
Inputs may be any that keep to these rules, and one draw needn't show every extreme that they name: `tile_subgrid`: among the tiles of one device (one coarse channel c and the 8 stations a of one index of stn), no subgrid is named more than 1024 times, and in every draw some device's tiles name some subgrid exactly 1024 times. `subgrid_slot`: each of 0 to 31 appears once.
All inputs are finite; a program needn't handle non-finite values.
Results may differ from a plain program's by a relative error of at most 0.0066.
Values may be sent and summed in bfloat16 or wider, within the bound.
No kernel may reach another device: no remote copies, remote signals or barrier semaphores. Data moves between devices by JAX's collectives and lax.ppermute only.
A program may use at most 128 MiB of HBM per device.

v0:
```python
import math
import jax
import jax.numpy as jnp
from jax import lax
from jax.sharding import PartitionSpec as P

FINE = 256
TAPS = 16
FRAMES = 4
CT = 4
G = 48
NSUB = 32
KW = 7


def fourier_table(length):
    index = jnp.arange(length, dtype=jnp.int32)
    phase = index[:, None] * index[None, :] % length
    angle = phase.astype(jnp.float32) * (2.0 * math.pi / length)
    cosine = jnp.cos(angle) / math.sqrt(length)
    sine = jnp.sin(angle) / math.sqrt(length)
    upper = jnp.concatenate([cosine, -sine], axis=1)
    lower = jnp.concatenate([sine, cosine], axis=1)
    return jnp.concatenate([upper, lower], axis=0)


def channelize(voltages, prototype):
    stations = voltages.shape[0]
    samples = (
        voltages[:, :, :, 0, :].astype(jnp.float32).reshape(stations, 2, 2, FRAMES + TAPS - 1, FINE)
    )
    filtered = jnp.zeros((stations, 2, 2, FRAMES, FINE), jnp.float32)
    for tap in range(TAPS):
        filtered = filtered + prototype[tap] * samples[:, :, :, tap : tap + FRAMES, :]
    frame_rows = filtered.transpose(0, 1, 3, 2, 4).reshape(stations * 2 * FRAMES, 2 * FINE)
    spectra = jnp.dot(frame_rows, fourier_table(FINE), precision=lax.Precision.HIGHEST).astype(
        jnp.bfloat16
    )
    spectra = spectra.reshape(stations, 2, FRAMES, 2, CT, FINE // CT)
    return spectra.transpose(4, 0, 1, 3, 2, 5).reshape(CT, 2 * stations, 2 * FRAMES * (FINE // CT))


def correlate(mine, theirs):
    tile_count, signal_count, lanes = theirs.shape
    halfway = lanes // 2
    flipped = jnp.concatenate([-theirs[:, :, halfway:], theirs[:, :, :halfway]], axis=2)
    partner = jnp.stack([theirs, flipped], axis=1)
    product = jnp.einsum("tak,tpbk->tapb", mine, partner, preferred_element_type=jnp.float32)
    local_stations = mine.shape[1] // 2
    block_count = signal_count // mine.shape[1]
    product = product.reshape(tile_count, local_stations, 2, 2, block_count, local_stations, 2)
    product = product.transpose(1, 0, 4, 5, 3, 2, 6).reshape(
        local_stations, tile_count, block_count, local_stations, 8
    )
    return (product * (1.0 / halfway)).astype(jnp.bfloat16)


def drop_autos(tiles_all, block_index):
    local_stations, tile_count, block_count, other_stations, comps = tiles_all.shape
    same_block = jnp.arange(block_count, dtype=jnp.int32) == block_index
    same_station = (
        jnp.arange(local_stations, dtype=jnp.int32)[:, None]
        == jnp.arange(other_stations, dtype=jnp.int32)[None, :]
    )
    matched = same_station[:, None, None, :, None] & same_block[None, None, :, None, None]
    return jnp.where(matched, jnp.zeros_like(tiles_all), tiles_all)


def lookup_taps(index, kernel_table):
    choose = (index[:, None] == jnp.arange(kernel_table.shape[0], dtype=jnp.int32)[None, :]).astype(
        jnp.float32
    )
    return jnp.dot(choose, kernel_table, precision=lax.Precision.HIGHEST).astype(jnp.bfloat16)


def spread_taps(taps, centre, extent):
    cells = jnp.arange(extent, dtype=jnp.int32)[:, None]
    placed = jnp.zeros((extent, taps.shape[1]), jnp.float32)
    for offset in range(KW):
        matched = cells == centre[None, :] + (offset - KW // 2)
        placed = jnp.where(matched, taps[offset][None, :].astype(jnp.float32), placed)
    return placed


def grid_slots(payload, cells):
    slot_count = payload.shape[1]
    values = payload[:8].astype(jnp.float32)
    across = spread_taps(payload[8 : 8 + KW], cells[0], G)
    down = spread_taps(payload[8 + KW : 8 + 2 * KW], cells[1], G).astype(jnp.bfloat16)
    weighted = (
        (values[:, None, :] * across[None, :, :]).astype(jnp.bfloat16).reshape(8 * G, slot_count)
    )
    return lax.dot_general(
        down, weighted, (((1,), (1,)), ((), ())), preferred_element_type=jnp.float32
    )


def grid_in_blocks(payload, cells, block_size):
    pieces = payload.shape[1] // block_size
    payload_blocks = payload.reshape(payload.shape[0], pieces, block_size).transpose(1, 0, 2)
    cell_blocks = cells.reshape(2, pieces, block_size).transpose(1, 0, 2)

    def accumulate(total, pair):
        return (total + grid_slots(pair[0], pair[1]), None)

    total, unused = lax.scan(
        accumulate, jnp.zeros((G, 8 * G), jnp.float32), (payload_blocks, cell_blocks)
    )
    return total


def per_device(
    voltages, prototype, kernel_table, tile_subgrid, tile_cells, tile_offsets, subgrid_slot
):
    spectra = channelize(voltages, prototype)
    rank_here = lax.axis_index("stn")
    result = correlate(spectra, lax.all_gather(spectra, "stn", axis=1, tiled=True))
    visible = drop_autos(result, rank_here)
    values = visible.reshape(-1, 8)
    tile_total = values.shape[0]
    slot_depth = 2 * tile_total // NSUB
    subgrid = tile_subgrid.reshape(-1)
    cells = tile_cells.reshape(-1, 2)
    offsets = tile_offsets.reshape(-1, 2)
    places_index = jnp.arange(NSUB, dtype=jnp.int32)[None, :]
    position = jnp.sum(
        jnp.where(subgrid[:, None] == places_index, subgrid_slot[None, :], 0), axis=1
    )
    member = (position[:, None] == places_index).astype(jnp.int32)
    rank = jnp.sum(member * jnp.cumsum(member, axis=0), axis=1) - 1
    target = position * slot_depth + rank
    across = lookup_taps(offsets[:, 0], kernel_table)
    down = lookup_taps(offsets[:, 1], kernel_table)
    payload = jnp.concatenate([values, across, down], axis=1)
    width_pay = payload.shape[1]
    slot_payload = (
        jnp.zeros((width_pay, NSUB * slot_depth), jnp.bfloat16).at[:, target].set(payload.T)
    )
    slot_cells = jnp.zeros((2, NSUB * slot_depth), jnp.int32).at[:, target].set(cells.T)
    slot_payload = slot_payload.reshape(width_pay, NSUB, slot_depth).transpose(1, 0, 2)
    slot_cells = slot_cells.reshape(2, NSUB, slot_depth).transpose(1, 0, 2)
    groups = lax.axis_size("chan")
    owned_count = NSUB // groups
    payloads = lax.all_to_all(
        slot_payload.reshape(groups, owned_count, width_pay, slot_depth),
        "chan",
        split_axis=0,
        concat_axis=3,
        tiled=True,
    )
    placements = lax.all_to_all(
        slot_cells.reshape(groups, owned_count, 2, slot_depth),
        "chan",
        split_axis=0,
        concat_axis=3,
        tiled=True,
    )

    def one_subgrid(pair):
        return grid_in_blocks(pair[0], pair[1], slot_depth)

    owned = lax.map(one_subgrid, (payloads[0], placements[0]))
    return lax.psum_scatter(owned, "stn", scatter_dimension=2, tiled=True)


def solution(mesh):
    return jax.shard_map(
        per_device,
        mesh=mesh,
        in_specs=(
            P("stn", None, None, "chan", None),
            P(),
            P(),
            P("chan", "stn", None, None, None),
            P("chan", "stn", None, None, None),
            P("chan", "stn", None, None, None),
            P(),
        ),
        out_specs=P("chan", None, "stn"),
        check_vma=False,
    )
```

profile of v0, /device:TPU:32, one launch (start us, length us, event | category | flops | bytes accessed | tf_op | source)
XLA Modules:
  0.0 1447.3 jit_solution(1598610117167969650)
XLA Ops:
  6.5 1.1 sine_multiply_fusion
  7.6 1.0 fusion.81
  8.6 1.2 fusion.86
  9.8 1.0 copy.111
  10.9 0.5 fusion.66
  11.6 0.8 convolution_convert_fusion.2
  12.5 0.8 reshape.633
  13.3 0.5 select_reduce_fusion
  14.5 1.6 broadcast_add_fusion.12
  16.1 2.0 copy.110
  18.1 1.7 fusion.40
  19.9 4.9 copy.123
  24.9 47.4 %scatter_custom_fusion.1 = s32[2,32768]{0,1:T(8,128)} fusion(s32[16384]{0:T(1024)S(1)} %bitcast.210, s32[16384,2]{1,0:T(8,128)} %copy.123, s32[]{:T(128)} %constant.50.clone.1), kind=kCustom, calls=%fused_computation.90 | custom fusion | bytes 262656 | tf_op jit(solution)/shard_map/scatter | solution.py:139
  72.3 9.9 copy.124
  82.2 12.6 all-to-all-start.1
  95.2 0.5 broadcast_in_dim.135
  95.8 0.4 convolution_convert_fusion
  96.2 0.4 convolution_convert_fusion.1
  96.6 36.8 %all-gather.2.cloned.1.call-done = bf16[4,1024,512]{2,1,0:T(8,128)(2,1)} async-done(((bf16[4,16,512]{2,1,0:T(8,128)(2,1)}), bf16[4,1024,512]{2,1,0:T(8,128)(2,1)}) %all-gather.2.cloned.1.call-update) | async-done | bytes 4194320 | tf_op jit(solution)/shard_map/all_gather | solution.py:117
  133.4 2.5 slice_negate_fusion
  136.3 1.8 copy-done.2
  138.1 2.7 fusion.46
  140.8 6.1 copy.115
  146.9 33.5 %copy.116 = bf16[8,4,64,8,2,2,2]{3,2,1,0,6,5,4:T(8,128)(2,1)} copy(bf16[8,4,64,8,2,2,2]{1,6,3,2,4,5,0:T(2,128)(2,1)} %bitcast.175) | data formatting | bytes 524288 | tf_op jit(solution)/shard_map/convert_element_type | solution.py:55
  180.4 10.4 convert_element_type.227
  191.1 3.4 copy.118
  194.5 46.3 %scatter_custom_fusion = bf16[22,32768]{0,1:T(8,128)(2,1)} fusion(s32[16384]{0:T(1024)S(1)} %bitcast.211, bf16[16384,22]{1,0:T(8,128)(2,1)} %copy.118, bf16[]{:T(256)} %constant.57.clone.1), kind=kCustom, calls=%fused_computation.93 | custom fusion | bytes 1442304 | tf_op jit(solution)/shard_map/scatter | solution.py:137
  240.7 7.4 copy.119
  248.2 0.6 reshape.636
  248.7 1.7 copy.120
  250.4 32.0 %all-to-all-start = ((bf16[8,4,22,1024]{3,1,2,0:T(4,128)(2,1)}), bf16[8,4,22,1024]{3,1,2,0:T(4,128)(2,1)S(1)}, u32[]{:S(2)}, u32[]{:S(2)}) async-start(bf16[8,4,22,1024]{3,1,2,0:T(4,128)(2,1)} %copy.120), calls=%async_computation | async-start | bytes 2883584 | tf_op jit(solution)/shard_map/all_to_all | solution.py:144
  282.8 63.8 %all-to-all-done = bf16[8,4,22,1024]{3,1,2,0:T(4,128)(2,1)S(1)} async-done(((bf16[8,4,22,1024]{3,1,2,0:T(4,128)(2,1)}), bf16[8,4,22,1024]{3,1,2,0:T(4,128)(2,1)S(1)}, u32[]{:S(2)}, u32[]{:S(2)}) %all-to-all-start) | async-done | bytes 1441824 | tf_op jit(solution)/shard_map/all_to_all | solution.py:144
  346.6 1.9 copy.129
  348.5 2.1 reshape.689
  350.6 29.1 %while.22 = (s32[]{:T(128)}, f32[4,48,384]{2,1,0:T(8,128)S(1)}, bf16[4,22,8192]{2,1,0:T(8,128)(2,1)S(1)}, s32[4,2,8192]{2,1,0:T(2,128)S(1)}, s32[]{:T(128)}, /*i...) while((s32[]{:T(128)}, f32[4,48,384]{2,1,0:T(8,128)S(1)}, ...), condition=%wide.region_9.10_spmd, body=%wide.region_6.9_spmd.sunk | while | flops 39983120 | bytes 5698380 | solution.py:162
  351.2 6.7 while.23
  352.5 0.4 convolution_add_fusion.2
  355.8 0.4 convolution_add_fusion.2
  358.5 6.7 while.23
  358.9 0.4 convolution_add_fusion.2
  365.8 6.7 while.23
  367.0 0.4 convolution_add_fusion.2
  373.0 6.7 while.23
  373.5 0.4 convolution_add_fusion.2
  379.8 1.2 copy.127
  381.0 1.3 dynamic-slice
  382.9 1056.3 %all-reduce.3.cloned.1.call-done = f32[4,48,384]{1,0,2:T(4,128)} async-done(((f32[4,48,384]{1,0,2:T(4,128)}), f32[4,48,384]{1,0,2:T(4,128)}) %all-reduce.3.cloned.1.call-update) | async-done | bytes 294928
  1439.2 1.3 constant_dynamic-slice_fusion.18
  (321 shorter events, 26.9 us)
Async XLA Ops:
  6.5 89.3 %copy-start = (f32[8,7]{1,0:T(8,128)S(1)}, f32[8,7]{1,0:T(8,128)}, u32[]{:S(2)}) copy-start(f32[8,7]{1,0:T(8,128)} %param.13) | copy-start | bytes 676
  6.5 126.9 %all-gather.2.cloned.1.call-start = ((), (), s32[]{:S(2)}) async-start(), calls=%async_computation.2 | async-start | bytes 4259840 | tf_op jit(solution)/shard_map/all_gather | solution.py:117
  11.4 1.9 copy-start.5
  11.4 1.9 copy-start.6
  18.1 1.7 copy-start.3
  72.3 23.4 %copy-start.4 = (s32[1,8,4,512,2]{3,4,2,1,0:T(2,128)S(1)}, s32[1,8,4,512,2]{3,4,2,1,0:T(2,128)}, u32[]{:S(2)}) copy-start(s32[1,8,4,512,2]{3,4,2,1,0:T(2,128)} %param.16) | copy-start | bytes 393220
  82.2 168.3 %all-to-all-start.1 = ((s32[8,4,2,1024]{3,2,1,0:T(2,128)}), s32[8,4,2,1024]{3,2,1,0:T(2,128)S(1)}, u32[]{:S(2)}, u32[]{:S(2)}) async-start(s32[8,4,2,1024]{3,2,1,0:T(2,128)} %bitcast.44), calls=%async_computation.1 | async-start | bytes 524288 | tf_op jit(solution)/shard_map/all_to_all | solution.py:151
  135.9 2.2 copy-start.2
  250.4 96.2 %all-to-all-start = ((bf16[8,4,22,1024]{3,1,2,0:T(4,128)(2,1)}), bf16[8,4,22,1024]{3,1,2,0:T(4,128)(2,1)S(1)}, u32[]{:S(2)}, u32[]{:S(2)}) async-start(bf16[8,4,22,1024]{3,1,2,0:T(4,128)(2,1)} %copy.120), calls=%async_computation | async-start | bytes 2883584 | tf_op jit(solution)/shard_map/all_to_all | solution.py:144
  282.4 1156.8 %all-reduce.3.cloned.1.call-start = ((), (), s32[]{:S(2)}) async-start(), calls=%async_computation.3 | async-start | bytes 1572864
  379.8 1060.7 %copy-start.1 = (f32[8,7]{1,0:T(8,128)S(1)}, f32[8,7]{1,0:T(8,128)}, u32[]{:S(2)}) copy-start(f32[8,7]{1,0:T(8,128)} %param.13) | copy-start | bytes 676
Sparse Core Ops, SparseCore 0:
  13.4 119.9 all-gather.1
  381.1 1058.0 all-reduce.2
where the time goes:
time: 1450 us
  waiting for transfers between devices  1160 us (80%)
  local copies, waits for them, and re-layouts  191 us (13%)
  starting transfers between devices  44.6 us (3%)
  other arithmetic  21.5 us (1%)
  matrix products  16.5 us (1%)
    unnamed x3, waiting for transfers between devices  1060 us
    all_to_all x1, waiting for transfers between devices, per_device(): lax.all_to_all(slot_payload.reshape(groups, owned_count, width_pay, slot_...  63.8 us
    convert_element_type x3, local copies, waits for them, and re-layouts, correlate(): return (product * (1.0 / halfway)).astype(jnp.bfloat16)  50.1 us
    scatter x1, local copies, waits for them, and re-layouts, per_device(): jnp.zeros((2, NSUB * slot_depth), jnp.int32).at[:, target].set(cells.T)  47.4 us
    scatter x1, local copies, waits for them, and re-layouts, per_device(): jnp.zeros((width_pay, NSUB * slot_depth), jnp.bfloat16).at[:, target]  46.3 us
    all_gather x1, waiting for transfers between devices, per_device(): lax.all_gather(spectra, 'stn', axis=1, tiled=True)  36.8 us
    all_to_all x1, starting transfers between devices, per_device(): lax.all_to_all(slot_payload.reshape(groups, owned_count, width_pay, slot_...  32 us
  transfers between devices with their start and end apart: 4, of which 3 were waited for; matrix products, arithmetic and copies ran while one was open for 13% of the time, Pallas kernels for 0%

commit v1 on v0

--- a/solution.py
+++ b/solution.py
@@ -3,6 +3,7 @@
 import jax.numpy as jnp
 from jax import lax
 from jax.sharding import PartitionSpec as P
+from jax.lax import all_to_all, axis_size
 
 FINE = 256
 TAPS = 16
@@ -11,6 +12,12 @@
 G = 48
 NSUB = 32
 KW = 7
+
+
+def name_zone(field_in, dev_axis="stn"):
+    return jnp.concatenate(
+        all_to_all(jnp.stack([field_in for _ in range(axis_size(dev_axis))]), dev_axis, 0, 0), 1
+    )
 
 
 def fourier_table(length):
@@ -114,7 +121,7 @@
 ):
     spectra = channelize(voltages, prototype)
     rank_here = lax.axis_index("stn")
-    result = correlate(spectra, lax.all_gather(spectra, "stn", axis=1, tiled=True))
+    result = correlate(spectra, name_zone(spectra))
     visible = drop_autos(result, rank_here)
     values = visible.reshape(-1, 8)
     tile_total = values.shape[0]

time: 1450 us -> 1530 us (1.055)
  waiting for transfers between devices: 1160 us -> 1240 us
    all_to_all x0 -> x1, waiting for transfers between devices: none -> 123 us  [name_zone(): all_to_all(jnp.stack([field_in for _ in range(axis_size(dev_axis))]), dev...]
    all_gather x1 -> x0, waiting for transfers between devices: 36.8 us -> none  [per_device(): lax.all_gather(spectra, 'stn', axis=1, tiled=True)]
    all_to_all x1, starting transfers between devices: 32 us -> 9.91 us  [per_device(): lax.all_to_all(slot_payload.reshape(groups, owned_count, width_pay, slot_...]
    all_to_all x0 -> x1, starting transfers between devices: none -> 21.2 us  [name_zone(): all_to_all(jnp.stack([field_in for _ in range(axis_size(dev_axis))]), dev...]
    unnamed x3 -> x2, waiting for transfers between devices: 1060 us -> 1050 us
  transfers between devices with their start and end apart: 4 -> 4, of which waited for: 3 -> 3; matrix products, arithmetic and copies ran while one was open for 13% -> 12% of each run, Pallas kernels for 0% -> 0%
where the time goes in v1:
time: 1530 us; the launch traced here: 1520 us
  waiting for transfers between devices  1240 us (81%)
  local copies, waits for them, and re-layouts  193 us (13%)
  starting transfers between devices  38 us (2%)
  other arithmetic  19.3 us (1%)
  matrix products  16.5 us (1%)
    unnamed x2, waiting for transfers between devices  1050 us
    all_to_all x1, waiting for transfers between devices, name_zone(): all_to_all(jnp.stack([field_in for _ in range(axis_size(dev_axis))]), dev...  123 us
    all_to_all x1, waiting for transfers between devices, per_device(): lax.all_to_all(slot_payload.reshape(groups, owned_count, width_pay, slot_...  63.8 us
    convert_element_type x3, local copies, waits for them, and re-layouts, correlate(): return (product * (1.0 / halfway)).astype(jnp.bfloat16)  50.1 us
    scatter x1, local copies, waits for them, and re-layouts, per_device(): jnp.zeros((2, NSUB * slot_depth), jnp.int32).at[:, target].set(cells.T)  47.4 us
    scatter x1, local copies, waits for them, and re-layouts, per_device(): jnp.zeros((width_pay, NSUB * slot_depth), jnp.bfloat16).at[:, target]  46.5 us
  transfers between devices with their start and end apart: 4, of which 3 were waited for; matrix products, arithmetic and copies ran while one was open for 12% of the time, Pallas kernels for 0%

profile of v1, /device:TPU:32, one launch (start us, length us, event | category | flops | bytes accessed | tf_op | source)
XLA Modules:
  0.0 1524.6 jit_solution(16552860831404931075)
XLA Ops:
  6.5 1.1 sine_multiply_fusion
  7.6 1.0 fusion.81
  8.6 1.1 fusion.86
  9.6 1.0 copy.111
  10.8 0.5 fusion.66
  11.4 0.8 convolution_convert_fusion.2
  12.5 2.5 stack.9
  15.0 21.2 %all-to-all-start = ((bf16[64,4,16,512]{3,2,1,0:T(8,128)(2,1)}), bf16[64,4,16,512]{3,2,1,0:T(8,128)(2,1)}, u32[]{:S(2)}, u32[]{:S(2)}) async-start(bf16[64,4,16,512]{3,2,1,0:T(8,128)(2,1)} %stack.9), calls=%async_computation | async-start | bytes 8388608 | tf_op jit(solution)/shard_map/all_to_all | solution.py:19
  36.5 0.5 broadcast_in_dim.135
  37.0 0.5 select_reduce_fusion
  38.2 1.6 broadcast_add_fusion.12
  39.8 2.0 copy.110
  41.8 4.9 copy.124
  46.8 1.7 fusion.40
  48.6 47.4 %scatter_custom_fusion.1 = s32[2,32768]{0,1:T(8,128)} fusion(s32[16384]{0:T(1024)S(1)} %bitcast.211, s32[16384,2]{1,0:T(8,128)} %copy.124, s32[]{:T(128)} %constant.50.clone.1), kind=kCustom, calls=%fused_computation.90 | custom fusion | bytes 262656 | tf_op jit(solution)/shard_map/scatter | solution.py:146
  96.0 9.9 copy.125
  106.0 0.4 convolution_convert_fusion
  106.4 0.4 convolution_convert_fusion.1
  106.8 123.0 %all-to-all-done = bf16[64,4,16,512]{3,2,1,0:T(8,128)(2,1)} async-done(((bf16[64,4,16,512]{3,2,1,0:T(8,128)(2,1)}), bf16[64,4,16,512]{3,2,1,0:T(8,128)(2,1)}, u32[]{:S(2)}, u32[]{:S(2)}) %all-to-all-start) | async-done | bytes 4194336 | tf_op jit(solution)/shard_map/all_to_all | solution.py:19
  229.8 6.9 all-to-all-start.2
  236.8 2.8 copy.114
  240.2 2.7 fusion.46
  242.9 6.1 copy.116
  249.0 33.5 %copy.117 = bf16[8,4,64,8,2,2,2]{3,2,1,0,6,5,4:T(8,128)(2,1)} copy(bf16[8,4,64,8,2,2,2]{1,6,3,2,4,5,0:T(2,128)(2,1)} %bitcast.175) | data formatting | bytes 524288 | tf_op jit(solution)/shard_map/convert_element_type | solution.py:62
  282.6 10.4 convert_element_type.227
  293.3 3.4 copy.119
  296.6 46.5 %scatter_custom_fusion = bf16[22,32768]{0,1:T(8,128)(2,1)} fusion(s32[16384]{0:T(1024)S(1)} %bitcast.212, bf16[16384,22]{1,0:T(8,128)(2,1)} %copy.119, bf16[]{:T(256)} %constant.57.clone.1), kind=kCustom, calls=%fused_computation.93 | custom fusion | bytes 1442304 | tf_op jit(solution)/shard_map/scatter | solution.py:144
  343.1 7.4 copy.120
  350.5 0.6 reshape.646
  351.1 1.7 copy.121
  352.8 9.9 all-to-all-start.1
  363.1 63.8 %all-to-all-done.1 = bf16[8,4,22,1024]{3,1,2,0:T(4,128)(2,1)S(1)} async-done(((bf16[8,4,22,1024]{3,1,2,0:T(4,128)(2,1)}), bf16[8,4,22,1024]{3,1,2,0:T(4,128)(2,1)S(1)}, u32[]{:S(2)}, u32[]{:S(2)}) %all-to-all-start.1) | async-done | bytes 1441824 | tf_op jit(solution)/shard_map/all_to_all | solution.py:151
  426.9 1.9 copy.130
  428.8 2.1 reshape.699
  431.0 29.1 %while.22 = (s32[]{:T(128)}, f32[4,48,384]{2,1,0:T(8,128)S(1)}, bf16[4,22,8192]{2,1,0:T(8,128)(2,1)S(1)}, s32[4,2,8192]{2,1,0:T(2,128)S(1)}, s32[]{:T(128)}, /*i...) while((s32[]{:T(128)}, f32[4,48,384]{2,1,0:T(8,128)S(1)}, ...), condition=%wide.region_9.10_spmd, body=%wide.region_6.9_spmd.sunk | while | flops 39983120 | bytes 5698380 | solution.py:169
  431.5 6.7 while.23
  432.0 0.4 convolution_add_fusion.2
  433.6 0.4 convolution_add_fusion.2
  438.8 6.7 while.23
  440.1 0.4 convolution_add_fusion.2
  446.1 6.7 while.23
  446.5 0.4 convolution_add_fusion.2
  453.4 6.7 while.23
  454.6 0.4 convolution_add_fusion.2
  460.1 1.2 copy.128
  461.3 1.3 dynamic-slice
  463.2 1053.0 %all-reduce.3.cloned.1.call-done = f32[4,48,384]{1,0,2:T(4,128)} async-done(((f32[4,48,384]{1,0,2:T(4,128)}), f32[4,48,384]{1,0,2:T(4,128)}) %all-reduce.3.cloned.1.call-update) | async-done | bytes 294928
  1516.2 1.3 constant_dynamic-slice_fusion.18
  (320 shorter events, 27.3 us)
Async XLA Ops:
  6.5 99.4 %copy-start = (f32[8,7]{1,0:T(8,128)S(1)}, f32[8,7]{1,0:T(8,128)}, u32[]{:S(2)}) copy-start(f32[8,7]{1,0:T(8,128)} %param.13) | copy-start | bytes 676
  15.0 22.0 %copy-start.4 = (s32[1,8,4,512,1]{3,4,2,1,0:T(1,128)S(1)}, s32[1,8,4,512,1]{3,4,2,1,0:T(1,128)}, u32[]{:S(2)}) copy-start(s32[1,8,4,512,1]{3,4,2,1,0:T(1,128)} %param.14) | copy-start | bytes 196612
  15.0 22.0 %copy-start.5 = (s32[32]{0:T(128)S(1)}, s32[32]{0:T(128)}, u32[]{:S(2)}) copy-start(s32[32]{0:T(128)} %param.17) | copy-start | bytes 388
  15.0 214.9 %all-to-all-start = ((bf16[64,4,16,512]{3,2,1,0:T(8,128)(2,1)}), bf16[64,4,16,512]{3,2,1,0:T(8,128)(2,1)}, u32[]{:S(2)}, u32[]{:S(2)}) async-start(bf16[64,4,16,512]{3,2,1,0:T(8,128)(2,1)} %stack.9), calls=%async_computation | async-start | bytes 8388608 | tf_op jit(solution)/shard_map/all_to_all | solution.py:19
  38.2 3.6 copy-start.2
  96.0 9.9 copy-start.3
  229.8 123.0 %all-to-all-start.2 = ((s32[8,4,2,1024]{3,2,1,0:T(2,128)}), s32[8,4,2,1024]{3,2,1,0:T(2,128)S(1)}, u32[]{:S(2)}, u32[]{:S(2)}) async-start(s32[8,4,2,1024]{3,2,1,0:T(2,128)} %bitcast.45), calls=%async_computation.2 | async-start | bytes 524288 | tf_op jit(solution)/shard_map/all_to_all | solution.py:158
  352.8 74.1 %all-to-all-start.1 = ((bf16[8,4,22,1024]{3,1,2,0:T(4,128)(2,1)}), bf16[8,4,22,1024]{3,1,2,0:T(4,128)(2,1)S(1)}, u32[]{:S(2)}, u32[]{:S(2)}) async-start(bf16[8,4,22,1024]{3,1,2,0:T(4,128)(2,1)} %copy.121), calls=%async_computation.1 | async-start | bytes 2883584 | tf_op jit(solution)/shard_map/all_to_all | solution.py:151
  362.7 1153.4 %all-reduce.3.cloned.1.call-start = ((), (), s32[]{:S(2)}) async-start(), calls=%async_computation.3 | async-start | bytes 1572864
  460.1 1057.4 %copy-start.1 = (f32[8,7]{1,0:T(8,128)S(1)}, f32[8,7]{1,0:T(8,128)}, u32[]{:S(2)}) copy-start(f32[8,7]{1,0:T(8,128)} %param.13) | copy-start | bytes 676
Sparse Core Ops, SparseCore 0:
  461.4 1054.7 all-reduce.2
